TPU v7x, 32 devices: a whole 2x2x4 slice. The times are simulated.
32 devices in a mesh: ctx: 8 (over z, y), head: 4 (over x, core).
Axes of the slice: x: 2, y: 2, z: 4, core: 2. Of those that a mesh axis runs over, the one named last changes fastest.
Arguments:
- query: bfloat16 [2048, 4096], P('ctx', 'head'), may hold values from -6 to 6
- key: bfloat16 [2048, 4096], P('ctx', 'head'), may hold values from -6 to 6
- value: bfloat16 [2048, 4096], P('ctx', 'head'), may hold values from -6 to 6
- episode_lengths: int32 [8], replicated, may hold values from 1 to 1024, 2048 in all
- attn_gain: float32 [4096], P('head'), may hold values from 0.1 to 1.9
- out_weight: bfloat16 [4096, 3072], P('head', 'ctx'), may hold values from -0.09375 to 0.09375
- residual: bfloat16 [2048, 3072], P('ctx', 'head'), may hold values from -36 to 36
- norm_gain: float32 [3072], P('head'), may hold values from 0.1 to 1.9
- expert_ids: int32 [2048, 2], P('ctx'), may hold values from 0 to 7, all different within a row; in each aligned block of 256 rows (0 to 255, 256 to 511, ...) at most 96 rows name the same one
- route_weights: int32 [2048, 2], P('ctx'), may hold values from 4096 to 65535
- gate_weight: bfloat16 [8, 3072, 5120], P('ctx', None, 'head'), may hold values from -0.109375 to 0.109375
- up_weight: bfloat16 [8, 3072, 5120], P('ctx', None, 'head'), may hold values from -0.109375 to 0.109375
- down_weight: bfloat16 [8, 5120, 3072], P('ctx', 'head'), may hold values from -0.125 to 0.125
Outputs:
- layer_out: bfloat16 [2048, 3072], P('ctx', 'head')
Inputs may be any that keep to these rules, and one draw needn't show every extreme that they name: `expert_ids`: in the rows of one device (256 tokens) no expert is named by more than 96 rows, a bound that some block reaches; a row names two different experts.
All inputs are finite; a program needn't handle non-finite values.
Results may differ from a plain program's by a relative error of at most 0.012.
Values may be sent and summed in bfloat16 or wider, within the bound.
A program may use at most 128 MiB of HBM per device.

v0:
```python
import jax
import jax.numpy as jnp
from jax import lax
from jax.sharding import PartitionSpec as P

HEAD_DIM = 128
highest = lax.Precision.HIGHEST


def entering(value, axis, join, neutral):
    place = lax.axis_index(axis)
    gathered = jax.tree.map(
        lambda a, kind: lax.all_gather(a.astype(kind), axis), value, (jnp.bfloat16, jnp.bfloat16)
    )
    state = jax.tree.map(lambda a, e: jnp.zeros_like(a) + jnp.asarray(e, a.dtype), value, neutral)

    def one(step, state):
        return join(
            state,
            jax.tree.map(
                lambda a, own: lax.dynamic_index_in_dim(a, step, 0, False).astype(own.dtype),
                gathered,
                value,
            ),
        )

    return lax.fori_loop(0, place, one, state)


def episode_of(positions, lengths):
    starts = jnp.cumsum(lengths) - lengths
    return jnp.sum((starts[None, :] <= positions[:, None]).astype(jnp.int32), axis=1) - 1


def link_states(earlier, latter):
    marker = jnp.maximum(earlier[0], latter[0])
    joined = jnp.where(latter[0][0] > 0.0, latter[1], earlier[1] + latter[1])
    return (marker, joined)


def on_device(
    query,
    key,
    value,
    episode_lengths,
    attn_gain,
    out_weight,
    residual,
    norm_gain,
    expert_ids,
    route_weights,
    gate_weight,
    up_weight,
    down_weight,
):
    tok_rows = query.shape[0]
    head_size = HEAD_DIM
    heads_local = query.shape[1] // head_size
    own_index = lax.axis_index("ctx")
    ctx_count = lax.axis_size("ctx")
    positions = own_index * tok_rows + jnp.arange(tok_rows, dtype=jnp.int32)
    episode = episode_of(positions, episode_lengths)
    prior = episode_of(positions[:1] - 1, episode_lengths)[0]
    final = episode[-1]
    lifted_query = jax.nn.silu(query.astype(jnp.float32)).reshape(tok_rows, heads_local, head_size)
    lifted_key = jax.nn.silu(key.astype(jnp.float32)).reshape(tok_rows, heads_local, head_size)
    value_rows = value.astype(jnp.float32).reshape(tok_rows, heads_local, head_size)
    keep = (episode == final).astype(jnp.float32)
    state = jnp.einsum(
        "shd,she->hde", lifted_key * keep[:, None, None], value_rows, precision=highest
    )
    marker = (final != prior).astype(jnp.float32).reshape(1)
    blank = (jnp.zeros((1,), jnp.float32), jnp.zeros_like(state))
    carried = entering((marker, state), "ctx", link_states, blank)
    carry_state = carried[1]
    order = jnp.arange(tok_rows, dtype=jnp.int32)
    allowed = ((order[:, None] >= order[None, :]) & (episode[:, None] == episode[None, :])).astype(
        jnp.float32
    )
    scores = jnp.einsum("thd,shd->hts", lifted_query, lifted_key, precision=highest)
    inside = jnp.einsum("hts,shd->thd", scores * allowed[None], value_rows, precision=highest)
    outside = jnp.einsum("thd,hde->the", lifted_query, carry_state, precision=highest)
    attn = inside + outside * (episode == prior).astype(jnp.float32)[:, None, None]
    mean_square = jnp.mean(attn * attn, axis=2, keepdims=True)
    scaled = attn * lax.rsqrt(mean_square + 1e-06) * attn_gain.reshape(heads_local, head_size)
    headed = scaled.reshape(tok_rows, heads_local * head_size).astype(jnp.bfloat16)
    mixed_part = jnp.dot(
        headed,
        lax.all_gather(out_weight, "ctx", axis=1, tiled=True),
        preferred_element_type=jnp.float32,
    )
    width = mixed_part.shape[1]
    mixed_slice = lax.psum_scatter(
        mixed_part.astype(jnp.bfloat16), "head", scatter_dimension=1, tiled=True
    ).astype(jnp.float32)
    hidden_slice = residual.astype(jnp.float32) + mixed_slice
    squares = lax.psum(jnp.sum(hidden_slice * hidden_slice, axis=1), "head")
    normed = (hidden_slice * lax.rsqrt(squares / width + 1e-06)[:, None] * norm_gain).astype(
        jnp.bfloat16
    )
    experts_count = gate_weight.shape[0] * ctx_count
    capacity = 3 * tok_rows // experts_count
    flat_ids = expert_ids.reshape(-1)
    onehot = (flat_ids[:, None] == jnp.arange(experts_count, dtype=jnp.int32)[None, :]).astype(
        jnp.int32
    )
    slot = jnp.sum(jnp.cumsum(onehot, axis=0) * onehot, axis=1) - 1
    source_rows = jnp.repeat(normed, 2, axis=0)
    outgoing = (
        jnp.zeros((experts_count, capacity, normed.shape[1]), jnp.bfloat16)
        .at[flat_ids, slot]
        .set(source_rows)
    )
    raw_weights = route_weights.astype(jnp.float32)
    share = (raw_weights / jnp.sum(raw_weights, axis=1, keepdims=True)).reshape(-1)
    full_rows = lax.all_gather(
        lax.all_to_all(outgoing, "ctx", split_axis=0, concat_axis=0, tiled=True),
        "head",
        axis=2,
        tiled=True,
    )
    flat = full_rows.reshape(-1, full_rows.shape[2])
    gate = jnp.dot(flat, gate_weight[0], preferred_element_type=jnp.float32)
    up = jnp.dot(flat, up_weight[0], preferred_element_type=jnp.float32)
    gated = (jax.nn.silu(gate) * up).astype(jnp.bfloat16)
    partial_value = jnp.dot(gated, down_weight[0], preferred_element_type=jnp.float32).astype(
        jnp.bfloat16
    )
    answer_partial_value = partial_value.reshape(
        full_rows.shape[0], full_rows.shape[1], partial_value.shape[1]
    )
    returned = lax.all_to_all(answer_partial_value, "ctx", split_axis=0, concat_axis=0, tiled=True)
    picked = returned[flat_ids, slot].astype(jnp.float32)
    weighted = jnp.sum((picked * share[:, None]).reshape(tok_rows, 2, picked.shape[1]), axis=1)
    moe = lax.psum_scatter(
        weighted.astype(jnp.bfloat16), "head", scatter_dimension=1, tiled=True
    ).astype(jnp.float32)
    return (hidden_slice + moe).astype(jnp.bfloat16)


def solution(mesh):
    placed = (
        P("ctx", "head"),
        P("ctx", "head"),
        P("ctx", "head"),
        P(),
        P("head"),
        P("head", "ctx"),
        P("ctx", "head"),
        P("head"),
        P("ctx", None),
        P("ctx", None),
        P("ctx", None, "head"),
        P("ctx", None, "head"),
        P("ctx", "head", None),
    )
    return jax.shard_map(
        on_device, mesh=mesh, in_specs=placed, out_specs=P("ctx", "head"), check_vma=False
    )
```

profile of v0, /device:TPU:0, one launch (start us, length us, event | category | flops | bytes accessed | tf_op | source)
XLA Modules:
  0.0 521.8 jit_solution(17571287380999060670)
XLA Ops:
  8.6 1.3 fusion.50
  10.5 1.3 convert_multiply_fusion
  13.4 1.4 convolution_convert_fusion.1
  17.5 23.2 %all-reduce = bf16[8]{0:T(256)(128)(2,1)S(1)} all-reduce(bf16[8]{0:T(256)(128)(2,1)S(1)} %dynamic-update-slice), channel_id=1, replica_groups=mesh['ctx'=8,'head'=4] {'ctx'}, use_global_device_ids=true, to_apply=%add | all-reduce | flops 8 | bytes 32
  40.9 3.4 fusion.32
  44.3 22.6 %all-gather.9.cloned.1.call-done = bf16[64,128,128]{2,1,0:T(8,128)(2,1)} async-done(((bf16[8,128,128]{2,1,0:T(8,128)(2,1)}), bf16[64,128,128]{2,1,0:T(8,128)(2,1)}) %all-gather.9.cloned.1.call-update) | async-done | bytes 2097168 | tf_op jit(solution)/shard_map/all_gather | solution.py:13
  67.0 1.3 fusion.23
  68.6 1.5 multiply_reduce_fusion.1
  70.3 96.8 %all-gather.5.cloned.1.call-done = bf16[1024,3072]{1,0:T(8,128)(2,1)} async-done(((bf16[1024,384]{1,0:T(8,128)(2,1)}), bf16[1024,3072]{1,0:T(8,128)(2,1)}) %all-gather.5.cloned.1.call-update) | async-done | bytes 6291472 | tf_op jit(solution)/shard_map/all_gather | solution.py:89
  167.0 5.8 %convolution_convert_fusion = bf16[256,3072]{1,0:T(8,128)(2,1)} fusion(bf16[256,1024]{0,1:T(8,128)(2,1)S(1)} %bitcast.92, bf16[1024,3072]{1,0:T(8,128)(2,1)} %all-gather.5.cloned.1.call-done), kind=kOutput, calls=%fused_computation.13 | convolution fusion | flops 1611399168 | bytes 8388608 | tf_op jit(solution)/shard_map/dot_general | solution.py:87
  175.0 24.2 %reduce-scatter.3.cloned.1.call-done = bf16[256,768]{1,0:T(8,128)(2,1)} async-done(((bf16[256,3072]{1,0:T(8,128)(2,1)}), bf16[256,768]{1,0:T(8,128)(2,1)}) %reduce-scatter.3.cloned.1.call-update) | async-done | bytes 393232 | tf_op jit(solution)/shard_map/reduce_scatter | solution.py:93
  200.5 5.8 %psum.7 = f32[256]{0:T(256)S(1)} all-reduce(f32[256]{0:T(256)S(1)} %multiply_reduce_fusion.2), channel_id=1, replica_groups=mesh['ctx'=8,'head'=4] {'head'}, use_global_device_ids=true, to_apply=%region_11.12 | all-reduce | flops 256 | bytes 2048 | tf_op jit(solution)/shard_map/psum | solution.py:97
  208.2 30.3 %scatter_fusion = bf16[8,96,768]{2,1,0:T(8,128)(2,1)S(1)} fusion(bf16[8,96,768]{2,1,0:T(8,128)(2,1)S(1)} %broadcast_in_dim.7, s32[512]{0:T(512)S(1)} %bitcast.88, bf16[512,768]{1,0:T(8,128)(2,1)S(1)} %reshape.237), kind=kCustom, calls=%fused_computation.1 | custom fusion | bytes 2363392 | tf_op jit(solution)/shard_map/scatter | solution.py:112
  238.5 34.4 %all_to_all.10 = bf16[8,96,768]{2,1,0:T(8,128)(2,1)} all-to-all(bf16[8,96,768]{2,1,0:T(8,128)(2,1)S(1)} %scatter_fusion), channel_id=1, replica_groups=mesh['ctx'=8,'head'=4] {'ctx'}, dimensions={0} | all-to-all | bytes 2359296 | tf_op jit(solution)/shard_map/all_to_all | solution.py:117
  272.9 35.3 %all-gather.7.cloned.1.call-done = bf16[8,96,3072]{2,1,0:T(8,128)(2,1)} async-done(((bf16[8,96,768]{2,1,0:T(8,128)(2,1)}), bf16[8,96,3072]{2,1,0:T(8,128)(2,1)}) %all-gather.7.cloned.1.call-update) | async-done | bytes 4718608 | tf_op jit(solution)/shard_map/all_gather | solution.py:116
  308.3 11.7 %fusion.4 = f32[768,1280]{1,0:T(8,128)} fusion(bf16[768,3072]{1,0:T(8,128)(2,1)} %bitcast.98, bf16[1,3072,1280]{2,1,0:T(8,128)(2,1)} %param.25), kind=kOutput, calls=%fused_computation.8 | convolution fusion | flops 6039797760 | bytes 16515072 | tf_op jit(solution)/shard_map/dot_general | solution.py:123
  320.0 22.0 %fusion.6 = bf16[768,3072]{1,0:T(8,128)(2,1)} fusion(bf16[1,1280,3072]{2,1,0:T(8,128)(2,1)} %param.27, bf16[768,3072]{1,0:T(8,128)(2,1)} %bitcast.99, bf16[1,3072,1280]{2,1,0:T(8,128)(2,1)} %param.26, f32[768,1280]{1,0:T(8,128)} %fusion.4), kind=kOutput, calls=%fused_computation.11 | convolution fusion | flops 12087853056 | bytes 29097984 | tf_op jit(solution)/shard_map/dot_general | solution.py:126
  342.0 5.6 %all-to-all-start.1 = ((bf16[8,96,3072]{2,1,0:T(8,128)(2,1)}), bf16[8,96,3072]{2,1,0:T(8,128)(2,1)}, u32[]{:S(2)}, u32[]{:S(2)}) async-start(bf16[8,96,3072]{2,1,0:T(8,128)(2,1)} %bitcast.89), calls=%async_computation.2 | async-start | bytes 9437184 | tf_op jit(solution)/shard_map/all_to_all | solution.py:132
  348.1 104.5 %all-to-all-done.1 = bf16[8,96,3072]{2,1,0:T(8,128)(2,1)} async-done(((bf16[8,96,3072]{2,1,0:T(8,128)(2,1)}), bf16[8,96,3072]{2,1,0:T(8,128)(2,1)}, u32[]{:S(2)}, u32[]{:S(2)}) %all-to-all-start.1) | async-done | bytes 4718624 | tf_op jit(solution)/shard_map/all_to_all | solution.py:132
  452.6 15.1 %gather_fusion = bf16[512,3072]{1,0:T(8,128)(2,1)} fusion(bf16[8,96,3072]{2,1,0:T(8,128)(2,1)} %all-to-all-done.1, s32[512]{0:T(512)S(1)} %bitcast.87), kind=kCustom, calls=%fused_computation | custom fusion | bytes 6295552 | tf_op jit(solution)/shard_map/gather | solution.py:133
  467.7 7.8 %reshape.228 = f32[256,2,3072]{2,1,0:T(2,128)} reshape(bf16[512,3072]{1,0:T(8,128)(2,1)} %gather_fusion) | data formatting | bytes 9437184 | tf_op jit(solution)/shard_map/convert_element_type | solution.py:133
  475.6 11.5 %multiply_reduce_fusion = bf16[256,3072]{1,0:T(8,128)(2,1)} fusion(f32[256,2,3072]{2,1,0:T(2,128)} %reshape.228, f32[256,2]{1,0:T(8,128)S(1)} %copy.50), kind=kLoop, calls=%fused_computation.10 | loop fusion | flops 2359296 | bytes 7866368 | tf_op jit(solution)/shard_map/reduce_sum | solution.py:134
  487.1 26.2 %reduce-scatter.5.cloned.1.call-done = bf16[256,768]{1,0:T(8,128)(2,1)} async-done(((bf16[256,3072]{1,0:T(8,128)(2,1)}), bf16[256,768]{1,0:T(8,128)(2,1)}) %reduce-scatter.5.cloned.1.call-update) | async-done | bytes 393232 | tf_op jit(solution)/shard_map/reduce_scatter | solution.py:135
  513.4 1.9 add_convert_fusion
  (69 shorter events, 11.5 us)
Async XLA Ops:
  6.5 6.9 %copy-start = (bf16[256,1024]{1,0:T(8,128)(2,1)S(1)}, bf16[256,1024]{1,0:T(8,128)(2,1)}, u32[]{:S(2)}) copy-start(bf16[256,1024]{1,0:T(8,128)(2,1)} %param.17) | copy-start | bytes 1572868
  6.5 9.7 %copy-start.10 = (u32[32]{0:T(128)S(1)}, u32[32]{0:T(128)}, u32[]{:S(2)}) copy-start(u32[32]{0:T(128)} %constant.109) | copy-start | bytes 388
  6.5 34.3 %copy-start.9 = (bf16[256,1024]{1,0:T(8,128)(2,1)S(1)}, bf16[256,1024]{1,0:T(8,128)(2,1)}, u32[]{:S(2)}) copy-start(bf16[256,1024]{1,0:T(8,128)(2,1)} %param.15) | copy-start | bytes 1572868
  6.5 60.4 %all-gather.9.cloned.1.call-start = ((), (), s32[]{:S(2)}) async-start(), calls=%async_computation.8 | async-start | bytes 2359296 | tf_op jit(solution)/shard_map/all_gather | solution.py:13
  14.8 152.2 %all-gather.5.cloned.1.call-start = ((), (), s32[]{:S(2)}) async-start(), calls=%async_computation.4 | async-start | bytes 7077888 | tf_op jit(solution)/shard_map/all_gather | solution.py:89
  15.6 183.7 %reduce-scatter.3.cloned.1.call-start = ((), (), s32[]{:S(2)}) async-start(), calls=%async_computation.5 | async-start | bytes 1966080 | tf_op jit(solution)/shard_map/reduce_scatter | solution.py:93
  67.0 1.6 copy-start.4
  67.0 3.1 copy-start.6
  167.0 5.9 %copy-start.8 = (s32[256,2]{0,1:T(2,128)S(1)}, s32[256,2]{0,1:T(2,128)}, u32[]{:S(2)}) copy-start(s32[256,2]{0,1:T(2,128)} %param.23) | copy-start | bytes 6148
  167.0 32.2 %copy-start.2 = (bf16[256,768]{1,0:T(8,128)(2,1)S(1)}, bf16[256,768]{1,0:T(8,128)(2,1)}, u32[]{:S(2)}) copy-start(bf16[256,768]{1,0:T(8,128)(2,1)} %param.21) | copy-start | bytes 1179652
  167.0 39.2 %copy-start.7 = (f32[768]{0:T(1024)S(1)}, f32[768]{0:T(1024)}, u32[]{:S(2)}) copy-start(f32[768]{0:T(1024)} %param.22) | copy-start | bytes 9220
  172.9 135.4 %all-gather.7.cloned.1.call-start = ((), (), s32[]{:S(2)}) async-start(), calls=%async_computation.6 | async-start | bytes 5898240 | tf_op jit(solution)/shard_map/all_gather | solution.py:116
  342.0 5.9 %copy-start.5 = (s32[256,2]{0,1:T(2,128)S(1)}, s32[256,2]{0,1:T(2,128)}, u32[]{:S(2)}) copy-start(s32[256,2]{0,1:T(2,128)} %param.24) | copy-start | bytes 6148
  342.0 110.6 %all-to-all-start.1 = ((bf16[8,96,3072]{2,1,0:T(8,128)(2,1)}), bf16[8,96,3072]{2,1,0:T(8,128)(2,1)}, u32[]{:S(2)}, u32[]{:S(2)}) async-start(bf16[8,96,3072]{2,1,0:T(8,128)(2,1)} %bitcast.89), calls=%async_computation.2 | async-start | bytes 9437184 | tf_op jit(solution)/shard_map/all_to_all | solution.py:132
  347.7 165.7 %reduce-scatter.5.cloned.1.call-start = ((), (), s32[]{:S(2)}) async-start(), calls=%async_computation.7 | async-start | bytes 1966080 | tf_op jit(solution)/shard_map/reduce_scatter | solution.py:135
  467.7 47.5 %copy-start.1 = (bf16[256,1024]{1,0:T(8,128)(2,1)S(1)}, bf16[256,1024]{1,0:T(8,128)(2,1)}, u32[]{:S(2)}) copy-start(bf16[256,1024]{1,0:T(8,128)(2,1)} %param.17) | copy-start | bytes 1572868
  475.6 37.8 %copy-start.3 = (bf16[256,768]{1,0:T(8,128)(2,1)S(1)}, bf16[256,768]{1,0:T(8,128)(2,1)}, u32[]{:S(2)}) copy-start(bf16[256,768]{1,0:T(8,128)(2,1)} %reduce-scatter.3.cloned.1.call-done) | copy-start | bytes 1179652
Sparse Core Ops, SparseCore 0:
  14.9 51.9 all-gather.8
  69.0 98.0 all-gather.4
  173.0 26.2 reduce-scatter.2
  273.0 35.1 all-gather.6
  487.3 26.0 reduce-scatter.4
where the time goes:
time: 523 us; the launch traced here: 522 us
  waiting for transfers between devices  310 us (59%)
  blocking collectives  63.4 us (12%)
  local copies, waits for them, and re-layouts  58 us (11%)
  matrix products  47.1 us (9%)
  other arithmetic  21.5 us (4%)
  between operations  15.3 us (3%)
  starting transfers between devices  6.03 us (1%)
    all_to_all x1, waiting for transfers between devices, on_device(): lax.all_to_all(answer_partial_value, 'ctx', split_axis=0, concat_axis=0,...  104 us
    all_gather x1, waiting for transfers between devices, on_device(): lax.all_gather(out_weight, 'ctx', axis=1, tiled=True)  96.8 us
    all_gather x1, waiting for transfers between devices, on_device(): lax.all_gather(lax.all_to_all(outgoing, 'ctx', split_axis=0, concat_axis=...  35.3 us
    all_to_all x1, blocking collectives, on_device(): lax.all_to_all(outgoing, 'ctx', split_axis=0, concat_axis=0, tiled=True)  34.4 us
    scatter x1, local copies, waits for them, and re-layouts, on_device(): outgoing = jnp.zeros((experts_count, capacity, normed.shape[1]), jnp.bflo...  30.3 us
    reduce_scatter x1, waiting for transfers between devices, on_device(): lax.psum_scatter(weighted.astype(jnp.bfloat16), 'head', scatter_dimension...  26.2 us
    reduce_scatter x1, waiting for transfers between devices, on_device(): lax.psum_scatter(mixed_part.astype(jnp.bfloat16), 'head', scatter_dimensi...  24.2 us
    unnamed x1, blocking collectives  23.2 us
  transfers between devices with their start and end apart: 6, of which 6 were waited for; matrix products, arithmetic and copies ran while one was open for 2% of the time, Pallas kernels for 0%

commit v1 on v0

--- a/solution.py
+++ b/solution.py
@@ -1,3 +1,4 @@
+import functools
 import jax
 import jax.numpy as jnp
 from jax import lax
@@ -5,6 +6,28 @@
 
 HEAD_DIM = 128
 highest = lax.Precision.HIGHEST
+
+
+def do_scales(block_here, axis_no):
+    dev_count = lax.axis_size("head")
+    buffer = [block_here]
+    for w in range(1, dev_count):
+        buffer.append(
+            lax.ppermute(
+                buffer[w - 1],
+                "head",
+                perm=[(num, (num - 1) % dev_count) for num in range(dev_count)],
+            )
+        )
+    big = jnp.roll(
+        jnp.concatenate(buffer, axis=axis_no),
+        lax.axis_index("head") * block_here.shape[axis_no],
+        axis=axis_no,
+    )
+    return big
+
+
+direct_the_matrix = functools.partial(do_scales, axis_no=2)
 
 
 def entering(value, axis, join, neutral):
@@ -113,11 +136,8 @@
     )
     raw_weights = route_weights.astype(jnp.float32)
     share = (raw_weights / jnp.sum(raw_weights, axis=1, keepdims=True)).reshape(-1)
-    full_rows = lax.all_gather(
-        lax.all_to_all(outgoing, "ctx", split_axis=0, concat_axis=0, tiled=True),
-        "head",
-        axis=2,
-        tiled=True,
+    full_rows = direct_the_matrix(
+        lax.all_to_all(outgoing, "ctx", split_axis=0, concat_axis=0, tiled=True)
     )
     flat = full_rows.reshape(-1, full_rows.shape[2])
     gate = jnp.dot(flat, gate_weight[0], preferred_element_type=jnp.float32)

time: 523 us -> 559 us (1.069)
  local copies, waits for them, and re-layouts: 58 us -> 86.5 us
    ppermute x0 -> x3, waiting for transfers between devices: none -> 39.7 us  [do_scales(): lax.ppermute(buffer[w - 1], 'head', perm=[(num, (num - 1) % dev_count) fo...]
    all_gather x1 -> x0, waiting for transfers between devices: 35.3 us -> none  [on_device(): lax.all_gather(lax.all_to_all(outgoing, 'ctx', split_axis=0, concat_axis=...]
    scatter x1, local copies, waits for them, and re-layouts: 30.3 us -> 46.9 us  [on_device(): outgoing = jnp.zeros((experts_count, capacity, normed.shape[1]), jnp.bflo...]
    unnamed x26 -> x37, local copies, waits for them, and re-layouts: 1.8 us -> 8.71 us
  transfers between devices with their start and end apart: 6 -> 8, of which waited for: 6 -> 8; matrix products, arithmetic and copies ran while one was open for 2% -> 3% of each run, Pallas kernels for 0% -> 0%
where the time goes in v1:
time: 559 us; the launch traced here: 555 us
  waiting for transfers between devices  314 us (56%)
  local copies, waits for them, and re-layouts  86.5 us (15%)
  blocking collectives  63.1 us (11%)
  matrix products  45.7 us (8%)
  other arithmetic  21.6 us (4%)
  between operations  15.3 us (3%)
  starting transfers between devices  8.79 us (2%)
    all_to_all x1, waiting for transfers between devices, on_device(): lax.all_to_all(answer_partial_value, 'ctx', split_axis=0, concat_axis=0,...  106 us
    all_gather x1, waiting for transfers between devices, on_device(): lax.all_gather(out_weight, 'ctx', axis=1, tiled=True)  95.9 us
    scatter x1, local copies, waits for them, and re-layouts, on_device(): outgoing = jnp.zeros((experts_count, capacity, normed.shape[1]), jnp.bflo...  46.9 us
    ppermute x3, waiting for transfers between devices, do_scales(): lax.ppermute(buffer[w - 1], 'head', perm=[(num, (num - 1) % dev_count) fo...  39.7 us
    all_to_all x1, blocking collectives, on_device(): lax.all_to_all(outgoing, 'ctx', split_axis=0, concat_axis=0, tiled=True)  34.1 us
    reduce_scatter x1, waiting for transfers between devices, on_device(): lax.psum_scatter(weighted.astype(jnp.bfloat16), 'head', scatter_dimension...  26.1 us
    reduce_scatter x1, waiting for transfers between devices, on_device(): lax.psum_scatter(mixed_part.astype(jnp.bfloat16), 'head', scatter_dimensi...  24.3 us
    unnamed x1, blocking collectives  23.2 us
  transfers between devices with their start and end apart: 8, of which 8 were waited for; matrix products, arithmetic and copies ran while one was open for 3% of the time, Pallas kernels for 0%

profile of v1, /device:TPU:0, one launch (start us, length us, event | category | flops | bytes accessed | tf_op | source)
XLA Modules:
  0.0 555.2 jit_solution(4291294224453770735)
XLA Ops:
  17.5 23.2 %all-reduce = bf16[8]{0:T(256)(128)(2,1)S(1)} all-reduce(bf16[8]{0:T(256)(128)(2,1)S(1)} %dynamic-update-slice), channel_id=1, replica_groups=mesh['ctx'=8,'head'=4] {'ctx'}, use_global_device_ids=true, to_apply=%add | all-reduce | flops 8 | bytes 32
  40.9 4.5 fusion.31
  45.3 21.6 %all-gather.6.cloned.1.call-done = bf16[64,128,128]{2,1,0:T(8,128)(2,1)} async-done(((bf16[8,128,128]{2,1,0:T(8,128)(2,1)}), bf16[64,128,128]{2,1,0:T(8,128)(2,1)}) %all-gather.6.cloned.1.call-update) | async-done | bytes 2097168 | tf_op jit(solution)/shard_map/all_gather | solution.py:36
  67.0 2.5 fusion.22
  71.1 95.9 %all-gather.4.cloned.1.call-done = bf16[1024,3072]{1,0:T(8,128)(2,1)} async-done(((bf16[1024,384]{1,0:T(8,128)(2,1)}), bf16[1024,3072]{1,0:T(8,128)(2,1)}) %all-gather.4.cloned.1.call-update) | async-done | bytes 6291472 | tf_op jit(solution)/shard_map/all_gather | solution.py:112
  167.0 5.8 %convolution_convert_fusion = bf16[256,3072]{1,0:T(8,128)(2,1)} fusion(bf16[256,1024]{0,1:T(8,128)(2,1)S(1)} %bitcast.92, bf16[1024,3072]{1,0:T(8,128)(2,1)} %all-gather.4.cloned.1.call-done), kind=kOutput, calls=%fused_computation.13 | convolution fusion | flops 1611399168 | bytes 8388608 | tf_op jit(solution)/shard_map/dot_general | solution.py:110
  175.0 24.3 %reduce-scatter.3.cloned.1.call-done = bf16[256,768]{1,0:T(8,128)(2,1)} async-done(((bf16[256,3072]{1,0:T(8,128)(2,1)}), bf16[256,768]{1,0:T(8,128)(2,1)}) %reduce-scatter.3.cloned.1.call-update) | async-done | bytes 393232 | tf_op jit(solution)/shard_map/reduce_scatter | solution.py:116
  200.4 5.8 %psum.7 = f32[256]{0:T(256)S(1)} all-reduce(f32[256]{0:T(256)S(1)} %multiply_reduce_fusion.2), channel_id=1, replica_groups=mesh['ctx'=8,'head'=4] {'head'}, use_global_device_ids=true, to_apply=%region_11.12 | all-reduce | flops 256 | bytes 2048 | tf_op jit(solution)/shard_map/psum | solution.py:120
  209.0 46.9 %scatter_fusion = bf16[8,96,768]{2,1,0:T(8,128)(2,1)S(1)} fusion(bf16[8,96,768]{2,1,0:T(8,128)(2,1)S(1)} %broadcast_in_dim.7, s32[512]{0:T(512)S(1)} %bitcast.86, bf16[512,768]{1,0:T(8,128)(2,1)} %reshape.237), kind=kCustom, calls=%fused_computation.1 | custom fusion | bytes 2363392 | tf_op jit(solution)/shard_map/scatter | solution.py:135
  256.0 34.1 %all_to_all.10 = bf16[8,96,768]{2,1,0:T(8,128)(2,1)S(1)} all-to-all(bf16[8,96,768]{2,1,0:T(8,128)(2,1)S(1)} %scatter_fusion), channel_id=1, replica_groups=mesh['ctx'=8,'head'=4] {'ctx'}, dimensions={0} | all-to-all | bytes 2359296 | tf_op jit(solution)/shard_map/all_to_all | solution.py:140
  290.1 13.7 %collective-permute-done = bf16[8,96,768]{2,1,0:T(8,128)(2,1)S(1)} collective-permute-done((bf16[8,96,768]{2,1,0:T(8,128)(2,1)S(1)}, bf16[8,96,768]{2,1,0:T(8,128)(2,1)S(1)}, u32[]{:S(2)}, u32[]{:S(2)}) %collective-permute-start) | collective-permute-done | bytes 1179680 | tf_op jit(solution)/shard_map/ppermute | solution.py:16
  305.7 13.7 %collective-permute-done.1 = bf16[8,96,768]{2,1,0:T(8,128)(2,1)} collective-permute-done((bf16[8,96,768]{2,1,0:T(8,128)(2,1)S(1)}, bf16[8,96,768]{2,1,0:T(8,128)(2,1)}, u32[]{:S(2)}, u32[]{:S(2)}) %collective-permute-start.1) | collective-permute-done | bytes 1179680 | tf_op jit(solution)/shard_map/ppermute | solution.py:16
  319.5 2.0 collective-permute-start.2
  323.2 12.3 %collective-permute-done.2 = bf16[8,96,768]{2,1,0:T(8,128)(2,1)} collective-permute-done((bf16[8,96,768]{2,1,0:T(8,128)(2,1)}, bf16[8,96,768]{2,1,0:T(8,128)(2,1)}, u32[]{:S(2)}, u32[]{:S(2)}) %collective-permute-start.2) | collective-permute-done | bytes 1179680 | tf_op jit(solution)/shard_map/ppermute | solution.py:16
  340.3 2.6 constant_dynamic-slice_fusion.1
  342.9 2.2 copy-done.2
  345.1 8.2 %fusion.4 = f32[768,1280]{1,0:T(8,128)} fusion(bf16[768,3072]{1,0:T(8,128)(2,1)S(1)} %bitcast.88, bf16[1,3072,1280]{2,1,0:T(8,128)(2,1)S(1)} %bitcast.99), kind=kOutput, calls=%fused_computation.8 | convolution fusion | flops 6039797760 | bytes 16515072 | tf_op jit(solution)/shard_map/dot_general | solution.py:143
  353.3 22.0 %fusion.6 = bf16[768,3072]{1,0:T(8,128)(2,1)} fusion(bf16[1,1280,3072]{2,1,0:T(8,128)(2,1)} %param.27, f32[768,1280]{1,0:T(8,128)} %fusion.4, bf16[768,3072]{1,0:T(8,128)(2,1)} %bitcast.89, bf16[1,3072,1280]{2,1,0:T(8,128)(2,1)} %param.26), kind=kOutput, calls=%fused_computation.11 | convolution fusion | flops 12087853056 | bytes 29097984 | tf_op jit(solution)/shard_map/dot_general | solution.py:146
  375.2 4.7 all-to-all-start.1
  380.2 105.9 %all-to-all-done.1 = bf16[8,96,3072]{2,1,0:T(8,128)(2,1)} async-done(((bf16[8,96,3072]{2,1,0:T(8,128)(2,1)}), bf16[8,96,3072]{2,1,0:T(8,128)(2,1)}, u32[]{:S(2)}, u32[]{:S(2)}) %all-to-all-start.1) | async-done | bytes 4718624 | tf_op jit(solution)/shard_map/all_to_all | solution.py:152
  486.1 15.1 %gather_fusion = bf16[512,3072]{1,0:T(8,128)(2,1)} fusion(bf16[8,96,3072]{2,1,0:T(8,128)(2,1)} %all-to-all-done.1, s32[512]{0:T(512)S(1)} %bitcast.85), kind=kCustom, calls=%fused_computation | custom fusion | bytes 6295552 | tf_op jit(solution)/shard_map/gather | solution.py:153
  501.3 7.8 %reshape.228 = f32[256,2,3072]{2,1,0:T(2,128)} reshape(bf16[512,3072]{1,0:T(8,128)(2,1)} %gather_fusion) | data formatting | bytes 9437184 | tf_op jit(solution)/shard_map/convert_element_type | solution.py:153
  509.1 11.5 %multiply_reduce_fusion = bf16[256,3072]{1,0:T(8,128)(2,1)} fusion(f32[256,2,3072]{2,1,0:T(2,128)} %reshape.228, f32[256,2]{1,0:T(8,128)S(1)} %copy.50), kind=kLoop, calls=%fused_computation.10 | loop fusion | flops 2359296 | bytes 7866368 | tf_op jit(solution)/shard_map/reduce_sum | solution.py:154
  520.7 26.1 %reduce-scatter.5.cloned.1.call-done = bf16[256,768]{1,0:T(8,128)(2,1)} async-done(((bf16[256,3072]{1,0:T(8,128)(2,1)}), bf16[256,768]{1,0:T(8,128)(2,1)}) %reduce-scatter.5.cloned.1.call-update) | async-done | bytes 393232 | tf_op jit(solution)/shard_map/reduce_scatter | solution.py:155
  (86 shorter events, 27.5 us)
Async XLA Ops:
  6.5 6.8 %copy-start = (bf16[256,1024]{1,0:T(8,128)(2,1)S(1)}, bf16[256,1024]{1,0:T(8,128)(2,1)}, u32[]{:S(2)}) copy-start(bf16[256,1024]{1,0:T(8,128)(2,1)} %param.17) | copy-start | bytes 1572868
  6.5 9.6 %copy-start.10 = (u32[32]{0:T(128)S(1)}, u32[32]{0:T(128)}, u32[]{:S(2)}) copy-start(u32[32]{0:T(128)} %constant.132) | copy-start | bytes 388
  6.5 60.4 %all-gather.6.cloned.1.call-start = ((), (), s32[]{:S(2)}) async-start(), calls=%async_computation.7 | async-start | bytes 2359296 | tf_op jit(solution)/shard_map/all_gather | solution.py:36
  14.8 152.2 %all-gather.4.cloned.1.call-start = ((), (), s32[]{:S(2)}) async-start(), calls=%async_computation.4 | async-start | bytes 7077888 | tf_op jit(solution)/shard_map/all_gather | solution.py:112
  15.5 183.7 %reduce-scatter.3.cloned.1.call-start = ((), (), s32[]{:S(2)}) async-start(), calls=%async_computation.5 | async-start | bytes 1966080 | tf_op jit(solution)/shard_map/reduce_scatter | solution.py:116
  66.9 2.5 copy-start.5
  67.0 4.0 copy-start.7
  167.0 5.8 %copy-start.9 = (s32[256,2]{0,1:T(2,128)S(1)}, s32[256,2]{0,1:T(2,128)}, u32[]{:S(2)}) copy-start(s32[256,2]{0,1:T(2,128)} %param.23) | copy-start | bytes 6148
  167.0 32.2 %copy-start.3 = (bf16[256,768]{1,0:T(8,128)(2,1)S(1)}, bf16[256,768]{1,0:T(8,128)(2,1)}, u32[]{:S(2)}) copy-start(bf16[256,768]{1,0:T(8,128)(2,1)} %param.21) | copy-start | bytes 1179652
  167.0 39.2 %copy-start.8 = (f32[768]{0:T(1024)S(1)}, f32[768]{0:T(1024)}, u32[]{:S(2)}) copy-start(f32[768]{0:T(1024)} %param.22) | copy-start | bytes 9220
  290.1 13.7 %collective-permute-start = (bf16[8,96,768]{2,1,0:T(8,128)(2,1)S(1)}, bf16[8,96,768]{2,1,0:T(8,128)(2,1)S(1)}, u32[]{:S(2)}, u32[]{:S(2)}) collective-permute-start(bf16[8,96,768]{2,1,0:T(8,128)(2,1)S(1)} %all_to_all.10), channel_id=1, source_target_pairs={{0,3},{1,0},{2,1},{3,2},{4,7},{5,4},{6,5},{7,6},{8,11},{9,8},{10,9... | collective-permute-start | bytes 3538952 | tf_op jit(solution)/shard_map/ppermute | solution.py:16
  303.8 15.6 %collective-permute-start.1 = (bf16[8,96,768]{2,1,0:T(8,128)(2,1)S(1)}, bf16[8,96,768]{2,1,0:T(8,128)(2,1)}, u32[]{:S(2)}, u32[]{:S(2)}) collective-permute-start(bf16[8,96,768]{2,1,0:T(8,128)(2,1)S(1)} %collective-permute-done), channel_id=1, source_target_pairs={{0,3},{1,0},{2,1},{3,2},{4,7},{5,4},{6,5},{7,6},{8,11},{9,8},{10,9... | collective-permute-start | bytes 3538952 | tf_op jit(solution)/shard_map/ppermute | solution.py:16
  319.5 16.0 %collective-permute-start.2 = (bf16[8,96,768]{2,1,0:T(8,128)(2,1)}, bf16[8,96,768]{2,1,0:T(8,128)(2,1)}, u32[]{:S(2)}, u32[]{:S(2)}) collective-permute-start(bf16[8,96,768]{2,1,0:T(8,128)(2,1)} %collective-permute-done.1), channel_id=1, source_target_pairs={{0,3},{1,0},{2,1},{3,2},{4,7},{5,4},{6,5},{7,6},{8,11},{9,8},{10,9... | collective-permute-start | bytes 3538952 | tf_op jit(solution)/shard_map/ppermute | solution.py:16
  337.3 7.8 %slice-start = ((s8[7864320]{0:T(1024)(128)(4,1)}), s8[4194304]{0:T(1024)(128)(4,1)S(1)}, s32[]{:S(2)}) async-start(s8[7864320]{0:T(1024)(128)(4,1)} %bitcast.98), calls=%async_computation.8 | async-start | bytes 8388608
  340.3 4.7 slice-start.1
  342.9 2.2 copy-start.2
  375.2 4.8 copy-start.6
  375.2 110.9 %all-to-all-start.1 = ((bf16[8,96,3072]{2,1,0:T(8,128)(2,1)}), bf16[8,96,3072]{2,1,0:T(8,128)(2,1)}, u32[]{:S(2)}, u32[]{:S(2)}) async-start(bf16[8,96,3072]{2,1,0:T(8,128)(2,1)} %bitcast.87), calls=%async_computation.2 | async-start | bytes 9437184 | tf_op jit(solution)/shard_map/all_to_all | solution.py:152
  380.0 166.8 %reduce-scatter.5.cloned.1.call-start = ((), (), s32[]{:S(2)}) async-start(), calls=%async_computation.6 | async-start | bytes 1966080 | tf_op jit(solution)/shard_map/reduce_scatter | solution.py:155
  501.3 47.4 %copy-start.1 = (bf16[256,1024]{1,0:T(8,128)(2,1)S(1)}, bf16[256,1024]{1,0:T(8,128)(2,1)}, u32[]{:S(2)}) copy-start(bf16[256,1024]{1,0:T(8,128)(2,1)} %param.17) | copy-start | bytes 1572868
  509.1 37.7 %copy-start.4 = (bf16[256,768]{1,0:T(8,128)(2,1)S(1)}, bf16[256,768]{1,0:T(8,128)(2,1)}, u32[]{:S(2)}) copy-start(bf16[256,768]{1,0:T(8,128)(2,1)} %reduce-scatter.3.cloned.1.call-done) | copy-start | bytes 1179652
Sparse Core Ops, SparseCore 0:
  14.9 51.9 all-gather.5
  69.0 98.0 all-gather.3
  173.0 26.2 reduce-scatter.2
  520.8 25.9 reduce-scatter.4
